TPU v7x, 512 devices: a whole 4x8x8 slice. The times are simulated.
512 devices in a mesh: rows: 32 (over y_hi, z, core), cols: 16 (over y_lo, x).
Axes of the slice: x: 4, y: 8 (y_hi: 2, y_lo: 4; y = y_hi * 4 + y_lo), z: 8, core: 2. Of those that a mesh axis runs over, the one named last changes fastest.
Arguments:
- jac: bfloat16 [32768, 1024], P(('rows', 'cols')), may hold values from -0.29882812 to 0.29882812
- panel_jac: bfloat16 [32768, 512], P(('rows', 'cols')), may hold values from -6 to 6
- weights: float32 [32768], P(('rows', 'cols')), may hold values from 0.1 to 1
- tile_lists: int32 [1024, 4], P(('rows', 'cols')), may hold values from 0 to 95, as said below
- tile_masks: int32 [1024, 4], P(('rows', 'cols')), may hold values from 0 to 1
- tile_order: int32 [96], replicated, may hold values from 0 to 95, as said below
- factor_inverse: float32 [512, 512], replicated, as said below
Outputs:
- panel_factor: float32 [96, 256, 512], P('cols', 'rows')
Inputs may be any that keep to these rules, and one draw needn't show every extreme that they name: `tile_order`: a permutation of 0 to 95. `tile_lists`: the 4 tiles of one row block are distinct; among the active slots of one device's 2 row blocks, at most 2 name tiles whose positions i share i // 6; in every draw every device has 2 such slots for one and the same position range. `factor_inverse`: lower triangular with a positive diagonal.
All inputs are finite; a program needn't handle non-finite values.
Results may differ from a plain program's by a relative error of at most 0.0029.
Values may be sent and summed in bfloat16 or wider, within the bound.
A program may use at most 64 MiB of HBM per device.

v0:
```python
import jax
import jax.numpy as jnp
from jax import lax
from jax.sharding import PartitionSpec as P


def tile_positions(tile_lists, tile_order):
    tile_count = tile_order.shape[0]
    matches = tile_lists[:, :, None] == tile_order[None, None, :]
    return jnp.sum(jnp.where(matches, jnp.arange(tile_count, dtype=jnp.int32), 0), axis=2)


def apply_inverse(tiles, factor_inverse):
    return jnp.einsum("ntp,qp->ntq", tiles, factor_inverse, precision=lax.Precision.HIGHEST)


def local(jac, panel_jac, weights, tile_lists, tile_masks, tile_order, factor_inverse):
    block_count, slot_count = tile_lists.shape
    block_rows = jac.shape[0] // block_count
    tile_width = jac.shape[1] // slot_count
    panel_width = panel_jac.shape[1]
    owners = lax.axis_size("cols")
    per_owner = tile_order.shape[0] // owners
    positions = tile_positions(tile_lists, tile_order)
    weighted = (weights[:, None] * panel_jac).astype(jnp.bfloat16)
    first_place = lax.axis_index("cols") * per_owner
    jac_piece = lax.all_gather(jac, "cols", axis=0, tiled=True)
    weighted_piece = lax.all_gather(weighted, "cols", axis=0, tiled=True)
    place_piece = lax.all_gather(positions, "cols", axis=0, tiled=True)
    mask_piece = lax.all_gather(tile_masks, "cols", axis=0, tiled=True)
    blocks_here = place_piece.shape[0]
    local_place = place_piece - first_place
    chosen = (
        (local_place[:, :, None] == jnp.arange(per_owner, dtype=jnp.int32))
        & (mask_piece[:, :, None] == 1)
    ).astype(jnp.bfloat16)
    columns = jac_piece.reshape(blocks_here, block_rows, slot_count, tile_width)
    mixed_tiles = jnp.einsum(
        "bkn,brkt->brnt", chosen, columns, preferred_element_type=jnp.float32
    ).astype(jnp.bfloat16)
    panels = weighted_piece.reshape(blocks_here, block_rows, panel_width)
    gram_tiles = jnp.einsum(
        "brnt,brp->ntp", mixed_tiles, panels, preferred_element_type=jnp.float32
    )
    reduced = lax.psum_scatter(gram_tiles, "rows", scatter_dimension=1, tiled=True)
    return apply_inverse(reduced, factor_inverse)


def solution(mesh):
    in_specs = (
        P(("rows", "cols"), None),
        P(("rows", "cols"), None),
        P(("rows", "cols")),
        P(("rows", "cols"), None),
        P(("rows", "cols"), None),
        P(),
        P(),
    )
    out_specs = P("cols", "rows", None)
    return jax.shard_map(local, mesh=mesh, in_specs=in_specs, out_specs=out_specs, check_vma=False)
```

profile of v0, /device:TPU:4, one launch (start us, length us, event | category | flops | bytes accessed | tf_op | source)
XLA Modules:
  0.0 340.9 jit_solution(16019776710534135513)
XLA Ops:
  6.5 0.0 copy-start
  6.5 0.0 all-gather.5.cloned.1.call-start
  6.5 0.7 all-gather.5.cloned.1.call-update
  7.3 0.0 all-gather.7.cloned.1.call-start
  7.3 1.5 multiply_convert_fusion
  8.9 0.0 all-gather.7.cloned.1.call-update
  8.9 0.0 reduce-scatter.2.cloned.1.call-start
  8.9 37.9 %all-gather.1 = s32[16,2,4]{2,1,0:T(2,128)S(1)} all-gather(s32[1,2,4]{2,1,0:T(2,128)} %bitcast.27), channel_id=1, replica_groups=mesh['rows'=32,'cols'=16] {'cols'}, dimensions={0}, use_global_device_ids=true | all-gather | bytes 544 | tf_op jit(solution)/shard_map/all_gather | solution.py:30
  46.8 0.1 copy.18
  46.9 0.1 copy.24
  47.1 0.9 select_reduce_fusion
  48.0 38.3 %all-gather = s32[16,2,4]{2,1,0:T(2,128)S(1)} all-gather(s32[1,2,4]{2,1,0:T(2,128)S(1)} %bitcast.26), channel_id=1, replica_groups=mesh['rows'=32,'cols'=16] {'cols'}, dimensions={0}, use_global_device_ids=true | all-gather | bytes 544 | tf_op jit(solution)/shard_map/all_gather | solution.py:29
  86.3 9.3 %all-gather.5.cloned.1.call-done = bf16[1024,1024]{1,0:T(8,128)(2,1)} async-done(((bf16[64,1024]{1,0:T(8,128)(2,1)}), bf16[1024,1024]{1,0:T(8,128)(2,1)}) %all-gather.5.cloned.1.call-update) | async-done | bytes 2097168 | tf_op jit(solution)/shard_map/all_gather | solution.py:27
  95.6 3.3 reshape.12
  98.9 3.2 convert_bitcast_fusion
  102.2 77.8 %all-gather.7.cloned.1.call-done = bf16[1024,512]{1,0:T(8,128)(2,1)} async-done(((bf16[64,512]{1,0:T(8,128)(2,1)}), bf16[1024,512]{1,0:T(8,128)(2,1)}) %all-gather.7.cloned.1.call-update) | async-done | bytes 1048592 | tf_op jit(solution)/shard_map/all_gather | solution.py:28
  179.9 6.0 %fusion.2 = f32[6,256,512]{2,1,0:T(8,128)} fusion(bf16[32,32,512,1]{2,1,0,3:T(8,128)(2,1)} %bitcast.28, bf16[32,32,6,256]{3,2,1,0:T(8,128)(2,1)} %convert_bitcast_fusion), kind=kOutput, calls=%fused_computation.3 | convolution fusion | flops 1610612736 | bytes 7340032 | tf_op jit(solution)/shard_map/brnt,brp->ntp/dot_general | solution.py:42
  186.0 0.0 reduce-scatter.2.cloned.1.call-update
  186.0 145.7 %reduce-scatter.2.cloned.1.call-done = f32[6,8,512]{2,1,0:T(8,128)} async-done(((f32[6,256,512]{2,1,0:T(8,128)}), f32[6,8,512]{2,1,0:T(8,128)}) %reduce-scatter.2.cloned.1.call-update) | async-done | bytes 98320 | tf_op jit(solution)/shard_map/reduce_scatter | solution.py:45
  331.7 0.0 copy-done
  331.7 2.6 fusion.5
  (3 shorter events, 0.0 us)
Async XLA Ops:
  6.5 325.2 %copy-start = (f32[512,512]{1,0:T(8,128)S(1)}, f32[512,512]{1,0:T(8,128)}, u32[]{:S(2)}) copy-start(f32[512,512]{1,0:T(8,128)} %param.13) | copy-start | bytes 3145732
  6.5 89.1 %all-gather.5.cloned.1.call-start = ((), (), s32[]{:S(2)}) async-start(), calls=%async_computation.1 | async-start | bytes 2228224 | tf_op jit(solution)/shard_map/all_gather | solution.py:27
  7.3 172.7 %all-gather.7.cloned.1.call-start = ((), (), s32[]{:S(2)}) async-start(), calls=%async_computation.2 | async-start | bytes 1114112 | tf_op jit(solution)/shard_map/all_gather | solution.py:28
  8.9 322.8 %reduce-scatter.2.cloned.1.call-start = ((), (), s32[]{:S(2)}) async-start(), calls=%async_computation.3 | async-start | bytes 3244032 | tf_op jit(solution)/shard_map/reduce_scatter | solution.py:45
Sparse Core Ops, SparseCore 0:
  9.4 86.1 all-gather.4
  97.7 82.2 all-gather.6
  186.1 145.5 reduce-scatter.1
where the time goes:
time: 341 us
  waiting for transfers between devices  234 us (69%)
  blocking collectives  76.2 us (22%)
  between operations  13.1 us (4%)
  matrix products  11.9 us (3%)
  local copies, waits for them, and re-layouts  3.56 us (1%)
    reduce_scatter x1, waiting for transfers between devices, local(): lax.psum_scatter(gram_tiles, 'rows', scatter_dimension=1, tiled=True)  146 us
    all_gather x1, waiting for transfers between devices, local(): weighted_piece = lax.all_gather(weighted, 'cols', axis=0, tiled=True)  77.8 us
    all_gather x1, blocking collectives, local(): place_piece = lax.all_gather(positions, 'cols', axis=0, tiled=True)  38.3 us
    all_gather x1, blocking collectives, local(): mask_piece = lax.all_gather(tile_masks, 'cols', axis=0, tiled=True)  37.9 us
    all_gather x1, waiting for transfers between devices, local(): jac_piece = lax.all_gather(jac, 'cols', axis=0, tiled=True)  9.29 us
  transfers between devices with their start and end apart: 3, of which 3 were waited for; matrix products, arithmetic and copies ran while one was open for 3% of the time, Pallas kernels for 0%

commit v1 on v0

--- a/solution.py
+++ b/solution.py
@@ -27,7 +27,8 @@
     jac_piece = lax.all_gather(jac, "cols", axis=0, tiled=True)
     weighted_piece = lax.all_gather(weighted, "cols", axis=0, tiled=True)
     place_piece = lax.all_gather(positions, "cols", axis=0, tiled=True)
-    mask_piece = lax.all_gather(tile_masks, "cols", axis=0, tiled=True)
+    sent = jnp.stack([tile_masks] * lax.axis_size("cols"))
+    mask_piece = jnp.concatenate(lax.all_to_all(sent, "cols", 0, 0), axis=0)
     blocks_here = place_piece.shape[0]
     local_place = place_piece - first_place
     chosen = (

time: 341 us -> 341 us (level)
  the two profiles are of different devices: /device:TPU:4 before, /device:TPU:2 now
where the time goes in v1:
time: 341 us
  waiting for transfers between devices  262 us (77%)
  blocking collectives  37.7 us (11%)
  between operations  13.1 us (4%)
  matrix products  11.9 us (3%)
  starting transfers between devices  9.25 us (3%)
  local copies, waits for them, and re-layouts  4.84 us (1%)
    reduce_scatter x1, waiting for transfers between devices, local(): lax.psum_scatter(gram_tiles, 'rows', scatter_dimension=1, tiled=True)  142 us
    all_gather x1, waiting for transfers between devices, local(): weighted_piece = lax.all_gather(weighted, 'cols', axis=0, tiled=True)  78 us
    all_gather x1, waiting for transfers between devices, local(): jac_piece = lax.all_gather(jac, 'cols', axis=0, tiled=True)  41.1 us
    all_gather x1, blocking collectives, local(): place_piece = lax.all_gather(positions, 'cols', axis=0, tiled=True)  37.7 us
    all_to_all x1, starting transfers between devices, local(): mask_piece = jnp.concatenate(lax.all_to_all(sent, 'cols', 0, 0), axis=0)  9.17 us
  transfers between devices with their start and end apart: 4, of which 3 were waited for; matrix products, arithmetic and copies ran while one was open for 3% of the time, Pallas kernels for 0%

profile of v1, /device:TPU:2, one launch (start us, length us, event | category | flops | bytes accessed | tf_op | source)
XLA Modules:
  0.0 340.8 jit_solution(5485587060489413828)
XLA Ops:
  6.5 0.0 copy-start
  6.5 0.0 all-gather.4.cloned.1.call-start
  6.5 0.7 all-gather.4.cloned.1.call-update
  7.3 0.0 all-gather.6.cloned.1.call-start
  7.3 1.5 multiply_convert_fusion
  8.9 0.0 all-gather.6.cloned.1.call-update
  8.9 1.3 stack.2
  10.2 9.2 %all-to-all-start = ((s32[16,2,4]{2,1,0:T(2,128)}), s32[16,2,4]{2,1,0:T(2,128)S(1)}, u32[]{:S(2)}, u32[]{:S(2)}) async-start(s32[16,2,4]{2,1,0:T(2,128)} %stack.2), calls=%async_computation | async-start | bytes 32768 | tf_op jit(solution)/shard_map/all_to_all | solution.py:31
  19.3 0.0 reduce-scatter.2.cloned.1.call-start
  19.4 0.9 select_reduce_fusion
  20.3 37.7 %all-gather = s32[16,2,4]{2,1,0:T(2,128)S(1)} all-gather(s32[1,2,4]{2,1,0:T(2,128)S(1)} %bitcast.25), channel_id=1, replica_groups=mesh['rows'=32,'cols'=16] {'cols'}, dimensions={0}, use_global_device_ids=true | all-gather | bytes 544 | tf_op jit(solution)/shard_map/all_gather | solution.py:29
  58.0 0.0 all-to-all-done
  58.0 0.1 copy.18
  58.1 0.1 copy.24
  58.2 41.1 %all-gather.4.cloned.1.call-done = bf16[1024,1024]{1,0:T(8,128)(2,1)} async-done(((bf16[64,1024]{1,0:T(8,128)(2,1)}), bf16[1024,1024]{1,0:T(8,128)(2,1)}) %all-gather.4.cloned.1.call-update) | async-done | bytes 2097168 | tf_op jit(solution)/shard_map/all_gather | solution.py:27
  99.3 3.3 reshape.21
  102.7 3.2 convert_bitcast_fusion
  105.9 78.0 %all-gather.6.cloned.1.call-done = bf16[1024,512]{1,0:T(8,128)(2,1)} async-done(((bf16[64,512]{1,0:T(8,128)(2,1)}), bf16[1024,512]{1,0:T(8,128)(2,1)}) %all-gather.6.cloned.1.call-update) | async-done | bytes 1048592 | tf_op jit(solution)/shard_map/all_gather | solution.py:28
  183.9 6.0 %fusion.2 = f32[6,256,512]{2,1,0:T(8,128)} fusion(bf16[32,32,512,1]{2,1,0,3:T(8,128)(2,1)} %bitcast.26, bf16[32,32,6,256]{3,2,1,0:T(8,128)(2,1)} %convert_bitcast_fusion), kind=kOutput, calls=%fused_computation.3 | convolution fusion | flops 1610612736 | bytes 7340032 | tf_op jit(solution)/shard_map/brnt,brp->ntp/dot_general | solution.py:43
  189.9 0.0 reduce-scatter.2.cloned.1.call-update
  189.9 141.7 %reduce-scatter.2.cloned.1.call-done = f32[6,8,512]{2,1,0:T(8,128)} async-done(((f32[6,256,512]{2,1,0:T(8,128)}), f32[6,8,512]{2,1,0:T(8,128)}) %reduce-scatter.2.cloned.1.call-update) | async-done | bytes 98320 | tf_op jit(solution)/shard_map/reduce_scatter | solution.py:46
  331.7 0.0 copy-done
  331.7 2.6 fusion.5
  (3 shorter events, 0.0 us)
Async XLA Ops:
  6.5 325.1 %copy-start = (f32[512,512]{1,0:T(8,128)S(1)}, f32[512,512]{1,0:T(8,128)}, u32[]{:S(2)}) copy-start(f32[512,512]{1,0:T(8,128)} %param.13) | copy-start | bytes 3145732
  6.5 92.8 %all-gather.4.cloned.1.call-start = ((), (), s32[]{:S(2)}) async-start(), calls=%async_computation.2 | async-start | bytes 2228224 | tf_op jit(solution)/shard_map/all_gather | solution.py:27
  7.3 176.6 %all-gather.6.cloned.1.call-start = ((), (), s32[]{:S(2)}) async-start(), calls=%async_computation.3 | async-start | bytes 1114112 | tf_op jit(solution)/shard_map/all_gather | solution.py:28
  10.2 47.8 %all-to-all-start = ((s32[16,2,4]{2,1,0:T(2,128)}), s32[16,2,4]{2,1,0:T(2,128)S(1)}, u32[]{:S(2)}, u32[]{:S(2)}) async-start(s32[16,2,4]{2,1,0:T(2,128)} %stack.2), calls=%async_computation | async-start | bytes 32768 | tf_op jit(solution)/shard_map/all_to_all | solution.py:31
  19.3 312.3 %reduce-scatter.2.cloned.1.call-start = ((), (), s32[]{:S(2)}) async-start(), calls=%async_computation.4 | async-start | bytes 3244032 | tf_op jit(solution)/shard_map/reduce_scatter | solution.py:46
Sparse Core Ops, SparseCore 0:
  9.4 89.8 all-gather.3
  101.4 82.3 all-gather.5
  190.0 141.5 reduce-scatter.1

commit v2 on v0

--- a/solution.py
+++ b/solution.py
@@ -24,8 +24,9 @@
     positions = tile_positions(tile_lists, tile_order)
     weighted = (weights[:, None] * panel_jac).astype(jnp.bfloat16)
     first_place = lax.axis_index("cols") * per_owner
-    jac_piece = lax.all_gather(jac, "cols", axis=0, tiled=True)
-    weighted_piece = lax.all_gather(weighted, "cols", axis=0, tiled=True)
+    arr_next = jnp.concatenate([jac, weighted], axis=1)
+    s_next = lax.all_gather(arr_next, "cols", axis=0, tiled=True)
+    jac_piece, weighted_piece = jnp.split(s_next, [jac.shape[1]], axis=1)
     place_piece = lax.all_gather(positions, "cols", axis=0, tiled=True)
     mask_piece = lax.all_gather(tile_masks, "cols", axis=0, tiled=True)
     blocks_here = place_piece.shape[0]

time: 341 us -> 265 us (0.78)
  the two profiles are of different devices: /device:TPU:4 before, /device:TPU:2 now
where the time goes in v2:
time: 265 us
  waiting for transfers between devices  154 us (58%)
  blocking collectives  80 us (30%)
  between operations  13.4 us (5%)
  matrix products  9.72 us (4%)
  local copies, waits for them, and re-layouts  4.58 us (2%)
  other arithmetic  3.51 us (1%)
    reduce_scatter x1, waiting for transfers between devices, local(): lax.psum_scatter(gram_tiles, 'rows', scatter_dimension=1, tiled=True)  142 us
    all_gather x1, blocking collectives, local(): mask_piece = lax.all_gather(tile_masks, 'cols', axis=0, tiled=True)  42.9 us
    all_gather x1, blocking collectives, local(): place_piece = lax.all_gather(positions, 'cols', axis=0, tiled=True)  37.2 us
    all_gather x1, waiting for transfers between devices, local(): s_next = lax.all_gather(arr_next, 'cols', axis=0, tiled=True)  12.2 us
  transfers between devices with their start and end apart: 2, of which 2 were waited for; matrix products, arithmetic and copies ran while one was open for 0% of the time, Pallas kernels for 0%

profile of v2, /device:TPU:2, one launch (start us, length us, event | category | flops | bytes accessed | tf_op | source)
XLA Modules:
  0.0 265.1 jit_solution(6126125571972361424)
XLA Ops:
  6.5 0.0 copy-start
  6.5 0.0 all-gather.4.cloned.1.call-start
  6.5 1.0 multiply_convert_fusion
  7.6 1.6 pad_maximum_fusion
  9.1 0.0 all-gather.4.cloned.1.call-update
  9.2 0.0 reduce-scatter.2.cloned.1.call-start
  9.2 42.9 %all-gather.1 = s32[16,2,4]{2,1,0:T(2,128)S(1)} all-gather(s32[1,2,4]{2,1,0:T(2,128)} %bitcast.28), channel_id=1, replica_groups=mesh['rows'=32,'cols'=16] {'cols'}, dimensions={0}, use_global_device_ids=true | all-gather | bytes 544 | tf_op jit(solution)/shard_map/all_gather | solution.py:31
  52.1 0.1 copy.18
  52.2 0.1 copy.24
  52.3 0.9 select_reduce_fusion
  53.2 37.2 %all-gather = s32[16,2,4]{2,1,0:T(2,128)S(1)} all-gather(s32[1,2,4]{2,1,0:T(2,128)S(1)} %bitcast.27), channel_id=1, replica_groups=mesh['rows'=32,'cols'=16] {'cols'}, dimensions={0}, use_global_device_ids=true | all-gather | bytes 544 | tf_op jit(solution)/shard_map/all_gather | solution.py:30
  90.4 12.2 %all-gather.4.cloned.1.call-done = bf16[1024,1536]{1,0:T(8,128)(2,1)} async-done(((bf16[64,1536]{1,0:T(8,128)(2,1)}), bf16[1024,1536]{1,0:T(8,128)(2,1)}) %all-gather.4.cloned.1.call-update) | async-done | bytes 3145744 | tf_op jit(solution)/shard_map/all_gather | solution.py:28
  102.6 0.0 slice-start
  102.6 1.6 slice-done
  104.2 2.8 %reshape.12 = bf16[32,32,4,256]{3,2,1,0:T(4,128)(2,1)} reshape(bf16[1024,1024]{1,0:T(8,128)(2,1)S(1)} %slice-done) | data formatting | bytes 4194304 | tf_op jit(solution)/shard_map/reshape | solution.py:38
  106.9 0.0 slice-start.1
  106.9 3.6 %convert_bitcast_fusion = bf16[32,32,6,256]{3,2,1,0:T(8,128)(2,1)S(1)} fusion(bf16[32,32,4,256]{3,2,1,0:T(4,128)(2,1)} %reshape.12, s32[32,4]{1,0:T(8,128)S(1)} %bitcast.25, pred[32,4]{1,0:T(8,128)(4,1)S(1)} %reshape.26), kind=kOutput, calls=%fused_computation | convolution fusion | flops 14157312 | bytes 5243520 | tf_op jit(solution)/shard_map/bkn,brkt->brnt/dot_general | solution.py:39
  110.5 0.0 slice-done.1
  110.5 3.5 %fusion.2 = f32[6,256,512]{2,1,0:T(8,128)} fusion(bf16[32,32,512,1]{2,1,0,3:T(8,128)(2,1)S(1)} %bitcast.24, bf16[32,32,6,256]{3,2,1,0:T(8,128)(2,1)S(1)} %convert_bitcast_fusion), kind=kOutput, calls=%fused_computation.3 | convolution fusion | flops 1610612736 | bytes 7340032 | tf_op jit(solution)/shard_map/brnt,brp->ntp/dot_general | solution.py:43
  114.1 0.0 reduce-scatter.2.cloned.1.call-update
  114.1 141.6 %reduce-scatter.2.cloned.1.call-done = f32[6,8,512]{2,1,0:T(8,128)} async-done(((f32[6,256,512]{2,1,0:T(8,128)}), f32[6,8,512]{2,1,0:T(8,128)}) %reduce-scatter.2.cloned.1.call-update) | async-done | bytes 98320 | tf_op jit(solution)/shard_map/reduce_scatter | solution.py:46
  255.7 0.0 copy-done
  255.7 2.6 fusion.5
  (3 shorter events, 0.0 us)
Async XLA Ops:
  6.5 249.1 %copy-start = (f32[512,512]{1,0:T(8,128)S(1)}, f32[512,512]{1,0:T(8,128)}, u32[]{:S(2)}) copy-start(f32[512,512]{1,0:T(8,128)} %param.13) | copy-start | bytes 3145732
  6.5 96.0 %all-gather.4.cloned.1.call-start = ((), (), s32[]{:S(2)}) async-start(), calls=%async_computation.1 | async-start | bytes 3342336 | tf_op jit(solution)/shard_map/all_gather | solution.py:28
  9.2 246.5 %reduce-scatter.2.cloned.1.call-start = ((), (), s32[]{:S(2)}) async-start(), calls=%async_computation.2 | async-start | bytes 3244032 | tf_op jit(solution)/shard_map/reduce_scatter | solution.py:46
  102.6 1.6 slice-start
  106.9 3.6 %slice-start.1 = ((bf16[1024,1536]{1,0:T(8,128)(2,1)}), bf16[1024,512]{1,0:T(8,128)(2,1)S(1)}, s32[]{:S(2)}) async-start(bf16[1024,1536]{1,0:T(8,128)(2,1)} %all-gather.4.cloned.1.call-done), calls=%async_computation.4 | async-start | bytes 2097152 | tf_op jit(solution)/shard_map/split | solution.py:29
Sparse Core Ops, SparseCore 0:
  9.4 93.1 all-gather.3
  114.2 141.4 reduce-scatter.1
